TPU v7x, 256 devices: a whole 4x4x8 slice. The times are simulated.
256 devices in a mesh: gx: 8 (over x, core), gy: 32 (over z, y).
Axes of the slice: x: 4, y: 4, z: 8, core: 2. Of those that a mesh axis runs over, the one named last changes fastest.
Arguments:
- residual: float32 [1024, 1024, 256], P('gx', 'gy'), may hold values from -6 to 6
- local_x: bfloat16 [136, 136], replicated, may hold values from -0.5 to 0.5
- local_y: bfloat16 [40, 40], replicated, may hold values from -1 to 1
- local_z: bfloat16 [256, 256], replicated, may hold values from -0.375 to 0.375
- eig_x: float32 [136], replicated, may hold values from 0.1 to 2
- eig_y: float32 [40], replicated, may hold values from 0.1 to 2
- eig_z: float32 [256], replicated, may hold values from 0.1 to 2
- coarse_x: bfloat16 [128, 4], replicated, may hold values from -0.5 to 0.5
- coarse_y: bfloat16 [32, 4], replicated, may hold values from -1 to 1
- coarse_z: bfloat16 [256, 4], replicated, may hold values from -0.375 to 0.375
- mode_x: float32 [32, 32], replicated, may hold values from -1 to 1
- mode_y: float32 [128, 128], replicated, may hold values from -0.5 to 0.5
- mode_z: float32 [4, 4], replicated, may hold values from -3 to 3
- coarse_eig_x: float32 [32], replicated, may hold values from 0.002 to 0.02
- coarse_eig_y: float32 [128], replicated, may hold values from 0.002 to 0.02
- coarse_eig_z: float32 [4], replicated, may hold values from 0.002 to 0.02
Outputs:
- preconditioned: float32 [1024, 1024, 256], P('gx', 'gy')
All inputs are finite; a program needn't handle non-finite values.
Results may differ from a plain program's by a relative error of at most 0.0045.
Values may be sent and summed in bfloat16 or wider, within the bound.
No kernel may reach another device: no remote copies, remote signals or barrier semaphores. Data moves between devices by JAX's collectives and lax.ppermute only.
A program may use at most 64 MiB of HBM per device.

v0:
```python
import jax
import jax.numpy as jnp
from jax import lax
from jax.sharding import PartitionSpec as P

OV = 4
MODES = 4


def with_halo(x, sides, width):
    for axis, dim in sides:
        size, length = (lax.axis_size(axis), x.shape[dim])
        up = [(i, (i + 1) % size) for i in range(size)]
        down = [(j, i) for i, j in up]
        last = lax.slice_in_dim(x, length - width, length, axis=dim)
        initial = lax.slice_in_dim(x, 0, width, axis=dim)
        before = lax.ppermute(last, axis, up)
        after = lax.ppermute(initial, axis, down)
        x = jnp.concatenate([before, x, after], axis=dim)
    return x


def solve_local(block, local_x, local_y, local_z, scales):
    first_x = jnp.einsum("xa,xyz->ayz", local_x, block, preferred_element_type=jnp.float32).astype(
        jnp.bfloat16
    )
    first_y = jnp.einsum(
        "yb,ayz->abz", local_y, first_x, preferred_element_type=jnp.float32
    ).astype(jnp.bfloat16)
    along = jnp.einsum("zc,abz->abc", local_z, first_y, preferred_element_type=jnp.float32)
    spectral = (along / scales).astype(jnp.bfloat16)
    back_z = jnp.einsum(
        "zc,abc->abz", local_z, spectral, preferred_element_type=jnp.float32
    ).astype(jnp.bfloat16)
    back_y = jnp.einsum("yb,abz->ayz", local_y, back_z, preferred_element_type=jnp.float32).astype(
        jnp.bfloat16
    )
    return jnp.einsum("xa,ayz->xyz", local_x, back_y, preferred_element_type=jnp.float32)


def strips_rows(field):
    return jnp.concatenate([field[:OV], field[field.shape[0] - OV :]], 0)


def strips_cols(field):
    return jnp.concatenate([field[:, :OV], field[:, field.shape[1] - OV :]], 1)


def add_rows(field, received):
    inner = field[OV : field.shape[0] - OV]
    inner = inner.at[:OV].add(received[:OV])
    return inner.at[inner.shape[0] - OV :].add(received[received.shape[0] - OV :])


def add_cols(field, received):
    inner = field[:, OV : field.shape[1] - OV]
    inner = inner.at[:, :OV].add(received[:, :OV])
    return inner.at[:, inner.shape[1] - OV :].add(received[:, received.shape[1] - OV :])


def local(
    residual,
    local_x,
    local_y,
    local_z,
    eig_x,
    eig_y,
    eig_z,
    coarse_x,
    coarse_y,
    coarse_z,
    mode_x,
    mode_y,
    mode_z,
    coarse_eig_x,
    coarse_eig_y,
    coarse_eig_z,
):
    cells_x, cells_y, levels = residual.shape
    rounded = residual.astype(jnp.bfloat16)
    along_z = jnp.dot(rounded.reshape(-1, levels), coarse_z, preferred_element_type=jnp.float32)
    along_z = along_z.reshape(cells_x, cells_y, MODES)
    basis_x = coarse_x.astype(jnp.float32)
    basis_y = coarse_y.astype(jnp.float32)
    own_coarse = jnp.einsum(
        "xyp,xm,yn->mnp", along_z, basis_x, basis_y, precision=lax.Precision.HIGHEST
    )
    row_index = lax.axis_index("gx")
    col_index = lax.axis_index("gy")
    rows_x = lax.dynamic_slice_in_dim(mode_x, row_index * MODES, MODES, 0)
    rows_y = lax.dynamic_slice_in_dim(mode_y, col_index * MODES, MODES, 0)
    partial_rows = lax.all_gather(own_coarse, "gx", axis=0, tiled=True)
    coarse_res = lax.all_gather(partial_rows, "gy", axis=1, tiled=True)
    coarse_hat = jnp.einsum(
        "IJp,Ia,Jb,pc->abc", coarse_res, mode_x, mode_y, mode_z, precision=lax.Precision.HIGHEST
    )
    coarse_hat = coarse_hat / (
        coarse_eig_x[:, None, None] + coarse_eig_y[None, :, None] + coarse_eig_z[None, None, :]
    )
    own_sol = jnp.einsum(
        "abc,ma,nb,pc->mnp", coarse_hat, rows_x, rows_y, mode_z, precision=lax.Precision.HIGHEST
    )
    spread = jnp.einsum(
        "mnp,xm,yn->xyp", own_sol, basis_x, basis_y, precision=lax.Precision.HIGHEST
    )
    coarse_fix = jnp.dot(
        spread.reshape(-1, MODES), coarse_z.astype(jnp.float32).T, precision=lax.Precision.HIGHEST
    )
    coarse_fix = coarse_fix.reshape(cells_x, cells_y, levels)
    extended = with_halo(rounded, (("gx", 0), ("gy", 1)), OV)
    scales = eig_x[:, None, None] + eig_y[None, :, None] + eig_z[None, None, :]
    local_fix = solve_local(extended, local_x, local_y, local_z, scales)
    received = with_halo(strips_rows(local_fix).astype(jnp.bfloat16), (("gx", 0),), OV).astype(
        jnp.float32
    )
    folded = add_rows(local_fix, received)
    received = with_halo(strips_cols(folded).astype(jnp.bfloat16), (("gy", 1),), OV).astype(
        jnp.float32
    )
    folded = add_cols(folded, received)
    return folded + coarse_fix


def solution(mesh):
    placed = (
        P("gx", "gy", None),
        P(),
        P(),
        P(),
        P(),
        P(),
        P(),
        P(),
        P(),
        P(),
        P(),
        P(),
        P(),
        P(),
        P(),
        P(),
    )
    return jax.shard_map(
        local, mesh=mesh, in_specs=placed, out_specs=P("gx", "gy", None), check_vma=False
    )
```

profile of v0, /device:TPU:1, one launch (start us, length us, event | category | flops | bytes accessed | tf_op | source)
XLA Modules:
  0.0 123.9 jit_solution(12545552153308260391)
XLA Ops:
  0.1 4.5 %copy.79 = bf16[128,32,256]{2,0,1:T(8,128)(2,1)S(1)} copy(f32[128,32,256]{2,1,0:T(8,128)} %param.24) | data formatting | bytes 6291456 | tf_op args[0]
  4.7 2.6 %collective-permute-start = (bf16[4,32,256]{2,0,1:T(4,128)(2,1)S(1)}, bf16[4,32,256]{2,0,1:T(4,128)(2,1)S(1)}, u32[]{:S(2)}, u32[]{:S(2)}) collective-permute-start(bf16[4,32,256]{2,0,1:T(4,128)(2,1)S(1)} %get-tuple-element.59), channel_id=1, source_target_pairs={{0,32},{32,64},{64,96},{96,128},{128,160},{160,192},{192,224},{224... | collective-permute-start | bytes 196616 | tf_op jit(solution)/shard_map/ppermute | solution.py:17
  7.3 0.6 collective-permute-start.1
  7.9 0.6 fusion.61
  9.1 15.5 %all_gather.6 = f32[32,4,4]{2,1,0:T(4,128)S(1)} all-gather(f32[4,4,4]{2,1,0:T(4,128)S(1)} %copy.28), channel_id=1, replica_groups=mesh['gx'=8,'gy'=32] {'gx'}, dimensions={0}, use_global_device_ids=true | all-gather | bytes 2304 | tf_op jit(solution)/shard_map/all_gather | solution.py:92
  24.7 38.5 %all_gather.7 = f32[32,128,4]{0,2,1:T(4,128)S(1)} all-gather(f32[32,4,4]{0,2,1:T(4,128)S(1)} %copy.29), channel_id=1, replica_groups=mesh['gx'=8,'gy'=32] {'gy'}, dimensions={1}, use_global_device_ids=true | all-gather | bytes 67584 | tf_op jit(solution)/shard_map/all_gather | solution.py:93
  63.3 0.4 convolution_bitcast_fusion.1
  64.3 0.3 fusion.44
  64.8 0.8 collective-permute-start.2
  65.6 4.0 %collective-permute-start.3 = (bf16[136,4,256]{2,0,1:T(8,128)(2,1)S(1)}, bf16[136,4,256]{2,0,1:T(8,128)(2,1)S(1)}, u32[]{:S(2)}, u32[]{:S(2)}) collective-permute-start(bf16[136,4,256]{2,0,1:T(8,128)(2,1)S(1)} %get-tuple-element.58), channel_id=1, source_target_pairs={{1,0},{2,1},{3,2},{4,3},{5,4},{6,5},{7,6},{8,7},{9,8},{10,9},{11,1... | collective-permute-start | bytes 835592 | tf_op jit(solution)/shard_map/ppermute | solution.py:18
  70.1 3.6 %collective-permute-done.2 = bf16[136,4,256]{2,0,1:T(8,128)(2,1)S(1)} collective-permute-done((bf16[136,4,256]{2,0,1:T(8,128)(2,1)S(1)}, bf16[136,4,256]{2,0,1:T(8,128)(2,1)S(1)}, u32[]{:S(2)}, u32[]{:S(2)}) %collective-permute-start.2) | collective-permute-done | bytes 278560 | tf_op jit(solution)/shard_map/ppermute | solution.py:17
  73.7 2.6 %convert_bitcast_fusion.1 = bf16[136,40,256]{2,0,1:T(8,128)(2,1)} fusion(bf16[136,4,256]{2,0,1:T(8,128)(2,1)S(1)} %collective-permute-done.3, bf16[4,32,256]{2,0,1:T(4,128)(2,1)S(1)} %collective-permute-done.1, bf16[128,32,256]{2,0,1:T(8,128)(2,1)S(1)} %copy.79, bf16[4,32,256]{2,0,1:T(4,128)(2,1)S(1)} %collective-permute-done, ...), kind=kOutput, calls=%fused_computation.22 | convolution fusion | flops 394117120 | bytes 5607552 | tf_op jit(solution)/shard_map/xa,xyz->ayz/dot_general | solution.py:24
  76.3 5.9 %fusion.10 = f32[136,40,256]{2,1,0:T(8,128)} fusion(bf16[136,40,256]{2,0,1:T(8,128)(2,1)} %convert_bitcast_fusion.1, bf16[256,256]{1,0:T(8,128)(2,1)S(1)} %copy-done, bf16[40,40]{1,0:T(8,128)(2,1)S(1)} %copy-done.4), kind=kOutput, calls=%fused_computation.12 | convolution fusion | flops 825835520 | bytes 8490112 | tf_op jit(solution)/shard_map/zc,abz->abc/dot_general | solution.py:30
  82.2 4.6 %convert_bitcast_fusion = bf16[136,40,256]{2,1,0:T(8,128)(2,1)S(1)} fusion(f32[136,40,256]{2,1,0:T(8,128)} %fusion.10, f32[256]{0:T(256)S(1)} %copy-done.13, f32[136,40]{1,0:T(8,128)S(1)} %broadcast_add_fusion, bf16[256,256]{1,0:T(8,128)(2,1)S(1)} %copy-done, bf16[40,40]{1,0:T(8,128)(2,1)S(1)} %copy-done.4), kind=kOutput, calls=%fused_computation.18 | convolution fusion | flops 831406080 | bytes 8512896 | tf_op jit(solution)/shard_map/yb,abz->ayz/dot_general | solution.py:35
  86.9 1.0 fusion.76
  87.9 13.8 %collective-permute-start.4 = (bf16[4,40,256]{2,0,1:T(4,128)(2,1)S(1)}, bf16[4,40,256]{2,0,1:T(4,128)(2,1)S(1)}, u32[]{:S(2)}, u32[]{:S(2)}) collective-permute-start(bf16[4,40,256]{2,0,1:T(4,128)(2,1)S(1)} %get-tuple-element.53), channel_id=1, source_target_pairs={{0,32},{32,64},{64,96},{96,128},{128,160},{160,192},{192,224},{224... | collective-permute-start | bytes 245768 | tf_op jit(solution)/shard_map/ppermute | solution.py:17
  101.9 0.7 slice.168
  102.6 0.5 collective-permute-done.4
  103.1 2.7 %collective-permute-done.5 = bf16[4,40,256]{2,0,1:T(4,128)(2,1)S(1)} collective-permute-done((bf16[4,40,256]{2,0,1:T(4,128)(2,1)S(1)}, bf16[4,40,256]{2,0,1:T(4,128)(2,1)S(1)}, u32[]{:S(2)}, u32[]{:S(2)}) %collective-permute-start.5) | collective-permute-done | bytes 81952 | tf_op jit(solution)/shard_map/ppermute | solution.py:18
  106.2 0.4 convert.13
  106.7 5.4 %collective-permute-start.7 = (bf16[128,4,256]{2,0,1:T(8,128)(2,1)S(1)}, bf16[128,4,256]{2,0,1:T(8,128)(2,1)S(1)}, u32[]{:S(2)}, u32[]{:S(2)}) collective-permute-start(bf16[128,4,256]{2,0,1:T(8,128)(2,1)S(1)} %get-tuple-element.56), channel_id=1, source_target_pairs={{1,0},{2,1},{3,2},{4,3},{5,4},{6,5},{7,6},{8,7},{9,8},{10,9},{11,1... | collective-permute-start | bytes 786440 | tf_op jit(solution)/shard_map/ppermute | solution.py:18
  112.8 4.7 %collective-permute-done.6 = bf16[128,4,256]{2,0,1:T(8,128)(2,1)S(1)} collective-permute-done((bf16[128,4,256]{2,0,1:T(8,128)(2,1)S(1)}, bf16[128,4,256]{2,0,1:T(8,128)(2,1)S(1)}, u32[]{:S(2)}, u32[]{:S(2)}) %collective-permute-start.6) | collective-permute-done | bytes 262176 | tf_op jit(solution)/shard_map/ppermute | solution.py:17
  117.6 1.9 %convolution_add_fusion = f32[128,32,256]{2,0,1:T(8,128)S(1)} fusion(f32[128,32,256]{2,0,1:T(8,128)S(1)} %fusion.31, f32[128,32,4]{0,1,2:T(8,128)S(1)} %convolution_bitcast_fusion, bf16[256,4]{0,1:T(4,128)(2,1)S(1)} %copy-done.5), kind=kOutput, calls=%fused_computation.25 | convolution fusion | flops 51380224 | bytes 8456192 | tf_op jit(solution)/shard_map/dot_general | solution.py:106
  119.5 4.4 %copy.40 = f32[128,32,256]{2,1,0:T(8,128)} copy(f32[128,32,256]{2,0,1:T(8,128)S(1)} %convolution_add_fusion) | data formatting | bytes 8388608 | tf_op jit(solution)/shard_map/add | solution.py:121
  (57 shorter events, 3.6 us)
Async XLA Ops:
  0.0 76.3 %copy-start = (bf16[256,256]{1,0:T(8,128)(2,1)S(1)}, bf16[256,256]{1,0:T(8,128)(2,1)}, u32[]{:S(2)}) copy-start(bf16[256,256]{1,0:T(8,128)(2,1)} %param.27) | copy-start | bytes 393220
  0.0 7.9 %copy-start.5 = (bf16[256,4]{0,1:T(4,128)(2,1)S(1)}, bf16[256,4]{0,1:T(4,128)(2,1)}, u32[]{:S(2)}) copy-start(bf16[256,4]{0,1:T(4,128)(2,1)} %param.33) | copy-start | bytes 6148
  0.0 8.6 %copy-start.6 = (bf16[128,4]{0,1:T(4,128)(2,1)S(1)}, bf16[128,4]{0,1:T(4,128)(2,1)}, u32[]{:S(2)}) copy-start(bf16[128,4]{0,1:T(4,128)(2,1)} %param.31) | copy-start | bytes 3076
  0.0 8.8 %copy-start.7 = (bf16[32,4]{0,1:T(4,128)(2,1)S(1)}, bf16[32,4]{0,1:T(4,128)(2,1)}, u32[]{:S(2)}) copy-start(bf16[32,4]{0,1:T(4,128)(2,1)} %param.32) | copy-start | bytes 772
  0.0 63.2 %copy-start.11 = (f32[128]{0:T(128)S(1)}, f32[128]{0:T(128)}, u32[]{:S(2)}) copy-start(f32[128]{0:T(128)} %param.38) | copy-start | bytes 1540
  0.0 63.2 %copy-start.12 = (f32[32]{0:T(128)S(1)}, f32[32]{0:T(128)}, u32[]{:S(2)}) copy-start(f32[32]{0:T(128)} %param.37) | copy-start | bytes 388
  0.0 63.3 %copy-start.3 = (f32[32,32]{1,0:T(8,128)S(1)}, f32[32,32]{1,0:T(8,128)}, u32[]{:S(2)}) copy-start(f32[32,32]{1,0:T(8,128)} %param.34) | copy-start | bytes 12292
  0.1 63.7 %copy-start.1 = (f32[128,128]{1,0:T(8,128)S(1)}, f32[128,128]{1,0:T(8,128)}, u32[]{:S(2)}) copy-start(f32[128,128]{1,0:T(8,128)} %param.35) | copy-start | bytes 196612
  0.1 63.9 %copy-start.8 = (f32[4,4]{1,0:T(4,128)S(1)}, f32[4,4]{1,0:T(4,128)}, u32[]{:S(2)}) copy-start(f32[4,4]{1,0:T(4,128)} %param.36) | copy-start | bytes 196
  0.1 63.9 %copy-start.14 = (f32[4]{0:T(128)S(1)}, f32[4]{0:T(128)}, u32[]{:S(2)}) copy-start(f32[4]{0:T(128)} %param.39) | copy-start | bytes 52
  4.6 65.4 %copy-start.9 = (f32[136]{0:T(256)S(1)}, f32[136]{0:T(256)}, u32[]{:S(2)}) copy-start(f32[136]{0:T(256)} %param.28) | copy-start | bytes 1636
  4.6 65.4 %copy-start.10 = (f32[40]{0:T(128)S(1)}, f32[40]{0:T(128)}, u32[]{:S(2)}) copy-start(f32[40]{0:T(128)} %param.29) | copy-start | bytes 484
  4.6 69.1 %copy-start.2 = (bf16[136,136]{1,0:T(8,128)(2,1)S(1)}, bf16[136,136]{1,0:T(8,128)(2,1)}, u32[]{:S(2)}) copy-start(bf16[136,136]{1,0:T(8,128)(2,1)} %param.25) | copy-start | bytes 110980
  4.7 59.9 %collective-permute-start = (bf16[4,32,256]{2,0,1:T(4,128)(2,1)S(1)}, bf16[4,32,256]{2,0,1:T(4,128)(2,1)S(1)}, u32[]{:S(2)}, u32[]{:S(2)}) collective-permute-start(bf16[4,32,256]{2,0,1:T(4,128)(2,1)S(1)} %get-tuple-element.59), channel_id=1, source_target_pairs={{0,32},{32,64},{64,96},{96,128},{128,160},{160,192},{192,224},{224... | collective-permute-start | bytes 196616 | tf_op jit(solution)/shard_map/ppermute | solution.py:17
  7.3 57.3 %collective-permute-start.1 = (bf16[4,32,256]{2,0,1:T(4,128)(2,1)S(1)}, bf16[4,32,256]{2,0,1:T(4,128)(2,1)S(1)}, u32[]{:S(2)}, u32[]{:S(2)}) collective-permute-start(bf16[4,32,256]{2,0,1:T(4,128)(2,1)S(1)} %get-tuple-element.60), channel_id=1, source_target_pairs={{32,0},{64,32},{96,64},{128,96},{160,128},{192,160},{224,192},{0,2... | collective-permute-start | bytes 196616 | tf_op jit(solution)/shard_map/ppermute | solution.py:18
  64.8 8.9 %collective-permute-start.2 = (bf16[136,4,256]{2,0,1:T(8,128)(2,1)S(1)}, bf16[136,4,256]{2,0,1:T(8,128)(2,1)S(1)}, u32[]{:S(2)}, u32[]{:S(2)}) collective-permute-start(bf16[136,4,256]{2,0,1:T(8,128)(2,1)S(1)} %get-tuple-element.57), channel_id=1, source_target_pairs={{0,1},{1,2},{2,3},{3,4},{4,5},{5,6},{6,7},{7,8},{8,9},{9,10},{10,1... | collective-permute-start | bytes 835592 | tf_op jit(solution)/shard_map/ppermute | solution.py:17
  65.6 8.1 %collective-permute-start.3 = (bf16[136,4,256]{2,0,1:T(8,128)(2,1)S(1)}, bf16[136,4,256]{2,0,1:T(8,128)(2,1)S(1)}, u32[]{:S(2)}, u32[]{:S(2)}) collective-permute-start(bf16[136,4,256]{2,0,1:T(8,128)(2,1)S(1)} %get-tuple-element.58), channel_id=1, source_target_pairs={{1,0},{2,1},{3,2},{4,3},{5,4},{6,5},{7,6},{8,7},{9,8},{10,9},{11,1... | collective-permute-start | bytes 835592 | tf_op jit(solution)/shard_map/ppermute | solution.py:18
  70.1 6.2 %copy-start.4 = (bf16[40,40]{1,0:T(8,128)(2,1)S(1)}, bf16[40,40]{1,0:T(8,128)(2,1)}, u32[]{:S(2)}) copy-start(bf16[40,40]{1,0:T(8,128)(2,1)} %param.26) | copy-start | bytes 9604
  76.3 5.9 %copy-start.13 = (f32[256]{0:T(256)S(1)}, f32[256]{0:T(256)}, u32[]{:S(2)}) copy-start(f32[256]{0:T(256)} %param.30) | copy-start | bytes 3076
  87.9 15.2 %collective-permute-start.4 = (bf16[4,40,256]{2,0,1:T(4,128)(2,1)S(1)}, bf16[4,40,256]{2,0,1:T(4,128)(2,1)S(1)}, u32[]{:S(2)}, u32[]{:S(2)}) collective-permute-start(bf16[4,40,256]{2,0,1:T(4,128)(2,1)S(1)} %get-tuple-element.53), channel_id=1, source_target_pairs={{0,32},{32,64},{64,96},{96,128},{128,160},{160,192},{192,224},{224... | collective-permute-start | bytes 245768 | tf_op jit(solution)/shard_map/ppermute | solution.py:17
  101.6 4.2 %collective-permute-start.5 = (bf16[4,40,256]{2,0,1:T(4,128)(2,1)S(1)}, bf16[4,40,256]{2,0,1:T(4,128)(2,1)S(1)}, u32[]{:S(2)}, u32[]{:S(2)}) collective-permute-start(bf16[4,40,256]{2,0,1:T(4,128)(2,1)S(1)} %get-tuple-element.54), channel_id=1, source_target_pairs={{32,0},{64,32},{96,64},{128,96},{160,128},{192,160},{224,192},{0,2... | collective-permute-start | bytes 245768 | tf_op jit(solution)/shard_map/ppermute | solution.py:18
  106.6 10.9 %collective-permute-start.6 = (bf16[128,4,256]{2,0,1:T(8,128)(2,1)S(1)}, bf16[128,4,256]{2,0,1:T(8,128)(2,1)S(1)}, u32[]{:S(2)}, u32[]{:S(2)}) collective-permute-start(bf16[128,4,256]{2,0,1:T(8,128)(2,1)S(1)} %get-tuple-element.55), channel_id=1, source_target_pairs={{0,1},{1,2},{2,3},{3,4},{4,5},{5,6},{6,7},{7,8},{8,9},{9,10},{10,1... | collective-permute-start | bytes 786440 | tf_op jit(solution)/shard_map/ppermute | solution.py:17
  106.7 10.8 %collective-permute-start.7 = (bf16[128,4,256]{2,0,1:T(8,128)(2,1)S(1)}, bf16[128,4,256]{2,0,1:T(8,128)(2,1)S(1)}, u32[]{:S(2)}, u32[]{:S(2)}) collective-permute-start(bf16[128,4,256]{2,0,1:T(8,128)(2,1)S(1)} %get-tuple-element.56), channel_id=1, source_target_pairs={{1,0},{2,1},{3,2},{4,3},{5,4},{6,5},{7,6},{8,7},{9,8},{10,9},{11,1... | collective-permute-start | bytes 786440 | tf_op jit(solution)/shard_map/ppermute | solution.py:18
where the time goes:
time: 124 us
  blocking collectives  54 us (44%)
  starting transfers between devices  27.3 us (22%)
  matrix products  19.1 us (15%)
  waiting for transfers between devices  11.5 us (9%)
  local copies, waits for them, and re-layouts  10.4 us (8%)
  other arithmetic  1.26 us (1%)
    all_gather x1, blocking collectives, local(): coarse_res = lax.all_gather(partial_rows, 'gy', axis=1, tiled=True)  38.5 us
    ppermute x4, starting transfers between devices, with_halo(): before = lax.ppermute(last, axis, up)  17.3 us
    all_gather x1, blocking collectives, local(): partial_rows = lax.all_gather(own_coarse, 'gx', axis=0, tiled=True)  15.5 us
    ppermute x4, starting transfers between devices, with_halo(): after = lax.ppermute(initial, axis, down)  10.1 us
    ppermute x4, waiting for transfers between devices, with_halo(): before = lax.ppermute(last, axis, up)  8.78 us
    dot_general x1, matrix products, solve_local(): jnp.einsum('zc,abz->abc', local_z, first_y, preferred_element_type=jnp.fl...  5.94 us
    dot_general x1, matrix products, solve_local(): jnp.einsum('yb,abz->ayz', local_y, back_z, preferred_element_type=jnp.flo...  4.64 us
    unnamed x31, local copies, waits for them, and re-layouts  4.63 us
  transfers between devices with their start and end apart: 8, of which 4 were waited for; matrix products, arithmetic and copies ran while one was open for 4% of the time, Pallas kernels for 0%

commit v1 on v0

--- a/solution.py
+++ b/solution.py
@@ -89,7 +89,10 @@
     col_index = lax.axis_index("gy")
     rows_x = lax.dynamic_slice_in_dim(mode_x, row_index * MODES, MODES, 0)
     rows_y = lax.dynamic_slice_in_dim(mode_y, col_index * MODES, MODES, 0)
-    partial_rows = lax.all_gather(own_coarse, "gx", axis=0, tiled=True)
+    peers = lax.axis_size("gx")
+    shards = jnp.stack([own_coarse for _ in range(peers)])
+    shards = lax.all_to_all(shards, "gx", split_axis=0, concat_axis=0)
+    partial_rows = jnp.concatenate(shards, axis=0)
     coarse_res = lax.all_gather(partial_rows, "gy", axis=1, tiled=True)
     coarse_hat = jnp.einsum(
         "IJp,Ia,Jb,pc->abc", coarse_res, mode_x, mode_y, mode_z, precision=lax.Precision.HIGHEST

time: 124 us -> 119 us (0.960)
  blocking collectives: 54 us -> 39.8 us
  starting transfers between devices: 27.3 us -> 33 us
  waiting for transfers between devices: 11.5 us -> 14.5 us
    all_gather x1 -> x0, blocking collectives: 15.5 us -> none  [local(): partial_rows = lax.all_gather(own_coarse, 'gx', axis=0, tiled=True)]
    all_to_all x0 -> x1, starting transfers between devices: none -> 6.44 us  [local(): shards = lax.all_to_all(shards, 'gx', split_axis=0, concat_axis=0)]
    all_to_all x0 -> x1, waiting for transfers between devices: none -> 2.97 us  [local(): shards = lax.all_to_all(shards, 'gx', split_axis=0, concat_axis=0)]
    all_gather x1, blocking collectives: 38.5 us -> 39.8 us  [local(): coarse_res = lax.all_gather(partial_rows, 'gy', axis=1, tiled=True)]
  transfers between devices with their start and end apart: 8 -> 9, of which waited for: 4 -> 5; matrix products, arithmetic and copies ran while one was open for 4% -> 3% of each run, Pallas kernels for 0% -> 0%
where the time goes in v1:
time: 119 us
  blocking collectives  39.8 us (33%)
  starting transfers between devices  33 us (28%)
  matrix products  19.2 us (16%)
  waiting for transfers between devices  14.5 us (12%)
  local copies, waits for them, and re-layouts  11.1 us (9%)
  other arithmetic  1.2 us (1%)
    all_gather x1, blocking collectives, local(): coarse_res = lax.all_gather(partial_rows, 'gy', axis=1, tiled=True)  39.8 us
    ppermute x4, starting transfers between devices, with_halo(): before = lax.ppermute(last, axis, up)  17 us
    ppermute x4, starting transfers between devices, with_halo(): after = lax.ppermute(initial, axis, down)  9.55 us
    ppermute x4, waiting for transfers between devices, with_halo(): before = lax.ppermute(last, axis, up)  8.81 us
    all_to_all x1, starting transfers between devices, local(): shards = lax.all_to_all(shards, 'gx', split_axis=0, concat_axis=0)  6.44 us
    dot_general x1, matrix products, solve_local(): jnp.einsum('zc,abz->abc', local_z, first_y, preferred_element_type=jnp.fl...  5.95 us
    dot_general x1, matrix products, solve_local(): jnp.einsum('yb,abz->ayz', local_y, back_z, preferred_element_type=jnp.flo...  4.64 us
    unnamed x31, local copies, waits for them, and re-layouts  4.61 us
  transfers between devices with their start and end apart: 9, of which 5 were waited for; matrix products, arithmetic and copies ran while one was open for 3% of the time, Pallas kernels for 0%

profile of v1, /device:TPU:1, one launch (start us, length us, event | category | flops | bytes accessed | tf_op | source)
XLA Modules:
  0.0 119.0 jit_solution(1453546534950071791)
XLA Ops:
  0.1 4.5 %copy.99 = bf16[128,32,256]{2,0,1:T(8,128)(2,1)S(1)} copy(f32[128,32,256]{2,1,0:T(8,128)} %param.24) | data formatting | bytes 6291456 | tf_op args[0]
  4.6 0.6 fusion.61
  5.8 0.6 stack.2
  6.5 6.4 %all-to-all-start = ((f32[8,4,4,4]{1,3,2,0:T(4,128)}), f32[8,4,4,4]{1,3,2,0:T(4,128)S(1)}, u32[]{:S(2)}, u32[]{:S(2)}) async-start(f32[8,4,4,4]{1,3,2,0:T(4,128)} %stack.2), calls=%async_computation | async-start | bytes 131072 | tf_op jit(solution)/shard_map/all_to_all | solution.py:94
  13.0 1.6 %collective-permute-start = (bf16[4,32,256]{2,0,1:T(4,128)(2,1)S(1)}, bf16[4,32,256]{2,0,1:T(4,128)(2,1)S(1)}, u32[]{:S(2)}, u32[]{:S(2)}) collective-permute-start(bf16[4,32,256]{2,0,1:T(4,128)(2,1)S(1)} %get-tuple-element.59), channel_id=1, source_target_pairs={{0,32},{32,64},{64,96},{96,128},{128,160},{160,192},{192,224},{224... | collective-permute-start | bytes 196616 | tf_op jit(solution)/shard_map/ppermute | solution.py:17
  14.8 3.0 %all-to-all-done = f32[8,4,4,4]{1,3,2,0:T(4,128)S(1)} async-done(((f32[8,4,4,4]{1,3,2,0:T(4,128)}), f32[8,4,4,4]{1,3,2,0:T(4,128)S(1)}, u32[]{:S(2)}, u32[]{:S(2)}) %all-to-all-start) | async-done | bytes 2080 | tf_op jit(solution)/shard_map/all_to_all | solution.py:94
  17.9 39.8 %all_gather.3 = f32[32,128,4]{0,2,1:T(4,128)S(1)} all-gather(f32[32,4,4]{0,2,1:T(4,128)S(1)} %reshape.196), channel_id=1, replica_groups=mesh['gx'=8,'gy'=32] {'gy'}, dimensions={1}, use_global_device_ids=true | all-gather | bytes 67584 | tf_op jit(solution)/shard_map/all_gather | solution.py:96
  57.7 0.4 convolution_bitcast_fusion.1
  58.8 0.7 collective-permute-start.2
  59.5 4.2 %collective-permute-start.3 = (bf16[136,4,256]{2,0,1:T(8,128)(2,1)S(1)}, bf16[136,4,256]{2,0,1:T(8,128)(2,1)S(1)}, u32[]{:S(2)}, u32[]{:S(2)}) collective-permute-start(bf16[136,4,256]{2,0,1:T(8,128)(2,1)S(1)} %get-tuple-element.58), channel_id=1, source_target_pairs={{1,0},{2,1},{3,2},{4,3},{5,4},{6,5},{7,6},{8,7},{9,8},{10,9},{11,1... | collective-permute-start | bytes 835592 | tf_op jit(solution)/shard_map/ppermute | solution.py:18
  64.4 3.3 %collective-permute-done.2 = bf16[136,4,256]{2,0,1:T(8,128)(2,1)S(1)} collective-permute-done((bf16[136,4,256]{2,0,1:T(8,128)(2,1)S(1)}, bf16[136,4,256]{2,0,1:T(8,128)(2,1)S(1)}, u32[]{:S(2)}, u32[]{:S(2)}) %collective-permute-start.2) | collective-permute-done | bytes 278560 | tf_op jit(solution)/shard_map/ppermute | solution.py:17
  67.7 2.6 %convert_bitcast_fusion.1 = bf16[136,40,256]{2,0,1:T(8,128)(2,1)} fusion(bf16[136,4,256]{2,0,1:T(8,128)(2,1)S(1)} %collective-permute-done.3, bf16[4,32,256]{2,0,1:T(4,128)(2,1)S(1)} %collective-permute-done.1, bf16[128,32,256]{2,0,1:T(8,128)(2,1)S(1)} %copy.99, bf16[4,32,256]{2,0,1:T(4,128)(2,1)S(1)} %collective-permute-done, ...), kind=kOutput, calls=%fused_computation.22 | convolution fusion | flops 394117120 | bytes 5607552 | tf_op jit(solution)/shard_map/xa,xyz->ayz/dot_general | solution.py:24
  70.3 6.0 %fusion.10 = f32[136,40,256]{2,1,0:T(8,128)} fusion(bf16[136,40,256]{2,0,1:T(8,128)(2,1)} %convert_bitcast_fusion.1, bf16[256,256]{1,0:T(8,128)(2,1)S(1)} %copy-done, bf16[40,40]{1,0:T(8,128)(2,1)S(1)} %copy-done.4), kind=kOutput, calls=%fused_computation.12 | convolution fusion | flops 825835520 | bytes 8490112 | tf_op jit(solution)/shard_map/zc,abz->abc/dot_general | solution.py:30
  76.3 4.6 %convert_bitcast_fusion = bf16[136,40,256]{2,1,0:T(8,128)(2,1)S(1)} fusion(f32[136,40,256]{2,1,0:T(8,128)} %fusion.10, f32[256]{0:T(256)S(1)} %copy-done.13, f32[136,40]{1,0:T(8,128)S(1)} %broadcast_add_fusion, bf16[256,256]{1,0:T(8,128)(2,1)S(1)} %copy-done, bf16[40,40]{1,0:T(8,128)(2,1)S(1)} %copy-done.4), kind=kOutput, calls=%fused_computation.18 | convolution fusion | flops 831406080 | bytes 8512896 | tf_op jit(solution)/shard_map/yb,abz->ayz/dot_general | solution.py:35
  80.9 1.0 fusion.76
  81.9 14.6 %collective-permute-start.4 = (bf16[4,40,256]{2,0,1:T(4,128)(2,1)S(1)}, bf16[4,40,256]{2,0,1:T(4,128)(2,1)S(1)}, u32[]{:S(2)}, u32[]{:S(2)}) collective-permute-start(bf16[4,40,256]{2,0,1:T(4,128)(2,1)S(1)} %get-tuple-element.53), channel_id=1, source_target_pairs={{0,32},{32,64},{64,96},{96,128},{128,160},{160,192},{192,224},{224... | collective-permute-start | bytes 245768 | tf_op jit(solution)/shard_map/ppermute | solution.py:17
  96.7 0.7 slice.168
  97.4 0.6 collective-permute-done.4
  98.0 2.7 %collective-permute-done.5 = bf16[4,40,256]{2,0,1:T(4,128)(2,1)S(1)} collective-permute-done((bf16[4,40,256]{2,0,1:T(4,128)(2,1)S(1)}, bf16[4,40,256]{2,0,1:T(4,128)(2,1)S(1)}, u32[]{:S(2)}, u32[]{:S(2)}) %collective-permute-start.5) | collective-permute-done | bytes 81952 | tf_op jit(solution)/shard_map/ppermute | solution.py:18
  101.1 0.4 convert.13
  101.5 5.4 %collective-permute-start.7 = (bf16[128,4,256]{2,0,1:T(8,128)(2,1)S(1)}, bf16[128,4,256]{2,0,1:T(8,128)(2,1)S(1)}, u32[]{:S(2)}, u32[]{:S(2)}) collective-permute-start(bf16[128,4,256]{2,0,1:T(8,128)(2,1)S(1)} %get-tuple-element.56), channel_id=1, source_target_pairs={{1,0},{2,1},{3,2},{4,3},{5,4},{6,5},{7,6},{8,7},{9,8},{10,9},{11,1... | collective-permute-start | bytes 786440 | tf_op jit(solution)/shard_map/ppermute | solution.py:18
  107.6 4.9 %collective-permute-done.6 = bf16[128,4,256]{2,0,1:T(8,128)(2,1)S(1)} collective-permute-done((bf16[128,4,256]{2,0,1:T(8,128)(2,1)S(1)}, bf16[128,4,256]{2,0,1:T(8,128)(2,1)S(1)}, u32[]{:S(2)}, u32[]{:S(2)}) %collective-permute-start.6) | collective-permute-done | bytes 262176 | tf_op jit(solution)/shard_map/ppermute | solution.py:17
  112.7 1.9 %convolution_add_fusion = f32[128,32,256]{2,0,1:T(8,128)S(1)} fusion(f32[128,32,256]{2,0,1:T(8,128)S(1)} %fusion.31, f32[128,32,4]{0,1,2:T(8,128)S(1)} %convolution_bitcast_fusion, bf16[256,4]{0,1:T(4,128)(2,1)S(1)} %copy-done.5), kind=kOutput, calls=%fused_computation.25 | convolution fusion | flops 51380224 | bytes 8456192 | tf_op jit(solution)/shard_map/dot_general | solution.py:109
  114.6 4.4 %copy.60 = f32[128,32,256]{2,1,0:T(8,128)} copy(f32[128,32,256]{2,0,1:T(8,128)S(1)} %convolution_add_fusion) | data formatting | bytes 8388608 | tf_op jit(solution)/shard_map/add | solution.py:124
  (60 shorter events, 3.9 us)
Async XLA Ops:
  0.0 70.3 %copy-start = (bf16[256,256]{1,0:T(8,128)(2,1)S(1)}, bf16[256,256]{1,0:T(8,128)(2,1)}, u32[]{:S(2)}) copy-start(bf16[256,256]{1,0:T(8,128)(2,1)} %param.27) | copy-start | bytes 393220
  0.0 4.6 %copy-start.5 = (bf16[256,4]{0,1:T(4,128)(2,1)S(1)}, bf16[256,4]{0,1:T(4,128)(2,1)}, u32[]{:S(2)}) copy-start(bf16[256,4]{0,1:T(4,128)(2,1)} %param.33) | copy-start | bytes 6148
  0.0 5.3 %copy-start.6 = (bf16[128,4]{0,1:T(4,128)(2,1)S(1)}, bf16[128,4]{0,1:T(4,128)(2,1)}, u32[]{:S(2)}) copy-start(bf16[128,4]{0,1:T(4,128)(2,1)} %param.31) | copy-start | bytes 3076
  0.0 5.5 %copy-start.7 = (bf16[32,4]{0,1:T(4,128)(2,1)S(1)}, bf16[32,4]{0,1:T(4,128)(2,1)}, u32[]{:S(2)}) copy-start(bf16[32,4]{0,1:T(4,128)(2,1)} %param.32) | copy-start | bytes 772
  0.0 14.6 %copy-start.10 = (f32[40]{0:T(128)S(1)}, f32[40]{0:T(128)}, u32[]{:S(2)}) copy-start(f32[40]{0:T(128)} %param.29) | copy-start | bytes 484
  0.0 14.6 %copy-start.9 = (f32[136]{0:T(256)S(1)}, f32[136]{0:T(256)}, u32[]{:S(2)}) copy-start(f32[136]{0:T(256)} %param.28) | copy-start | bytes 1636
  0.0 14.7 %copy-start.11 = (f32[128]{0:T(128)S(1)}, f32[128]{0:T(128)}, u32[]{:S(2)}) copy-start(f32[128]{0:T(128)} %param.38) | copy-start | bytes 1540
  0.1 14.7 %copy-start.12 = (f32[32]{0:T(128)S(1)}, f32[32]{0:T(128)}, u32[]{:S(2)}) copy-start(f32[32]{0:T(128)} %param.37) | copy-start | bytes 388
  0.1 57.6 %copy-start.3 = (f32[32,32]{1,0:T(8,128)S(1)}, f32[32,32]{1,0:T(8,128)}, u32[]{:S(2)}) copy-start(f32[32,32]{1,0:T(8,128)} %param.34) | copy-start | bytes 12292
  0.1 58.0 %copy-start.1 = (f32[128,128]{1,0:T(8,128)S(1)}, f32[128,128]{1,0:T(8,128)}, u32[]{:S(2)}) copy-start(f32[128,128]{1,0:T(8,128)} %param.35) | copy-start | bytes 196612
  0.1 58.2 %copy-start.8 = (f32[4,4]{1,0:T(4,128)S(1)}, f32[4,4]{1,0:T(4,128)}, u32[]{:S(2)}) copy-start(f32[4,4]{1,0:T(4,128)} %param.36) | copy-start | bytes 196
  0.1 58.2 %copy-start.14 = (f32[4]{0:T(128)S(1)}, f32[4]{0:T(128)}, u32[]{:S(2)}) copy-start(f32[4]{0:T(128)} %param.39) | copy-start | bytes 52
  4.6 63.1 %copy-start.2 = (bf16[136,136]{1,0:T(8,128)(2,1)S(1)}, bf16[136,136]{1,0:T(8,128)(2,1)}, u32[]{:S(2)}) copy-start(bf16[136,136]{1,0:T(8,128)(2,1)} %param.25) | copy-start | bytes 110980
  6.5 11.3 %all-to-all-start = ((f32[8,4,4,4]{1,3,2,0:T(4,128)}), f32[8,4,4,4]{1,3,2,0:T(4,128)S(1)}, u32[]{:S(2)}, u32[]{:S(2)}) async-start(f32[8,4,4,4]{1,3,2,0:T(4,128)} %stack.2), calls=%async_computation | async-start | bytes 131072 | tf_op jit(solution)/shard_map/all_to_all | solution.py:94
  13.0 45.7 %collective-permute-start = (bf16[4,32,256]{2,0,1:T(4,128)(2,1)S(1)}, bf16[4,32,256]{2,0,1:T(4,128)(2,1)S(1)}, u32[]{:S(2)}, u32[]{:S(2)}) collective-permute-start(bf16[4,32,256]{2,0,1:T(4,128)(2,1)S(1)} %get-tuple-element.59), channel_id=1, source_target_pairs={{0,32},{32,64},{64,96},{96,128},{128,160},{160,192},{192,224},{224... | collective-permute-start | bytes 196616 | tf_op jit(solution)/shard_map/ppermute | solution.py:17
  14.6 44.1 %collective-permute-start.1 = (bf16[4,32,256]{2,0,1:T(4,128)(2,1)S(1)}, bf16[4,32,256]{2,0,1:T(4,128)(2,1)S(1)}, u32[]{:S(2)}, u32[]{:S(2)}) collective-permute-start(bf16[4,32,256]{2,0,1:T(4,128)(2,1)S(1)} %get-tuple-element.60), channel_id=1, source_target_pairs={{32,0},{64,32},{96,64},{128,96},{160,128},{192,160},{224,192},{0,2... | collective-permute-start | bytes 196616 | tf_op jit(solution)/shard_map/ppermute | solution.py:18
  58.8 8.9 %collective-permute-start.2 = (bf16[136,4,256]{2,0,1:T(8,128)(2,1)S(1)}, bf16[136,4,256]{2,0,1:T(8,128)(2,1)S(1)}, u32[]{:S(2)}, u32[]{:S(2)}) collective-permute-start(bf16[136,4,256]{2,0,1:T(8,128)(2,1)S(1)} %get-tuple-element.57), channel_id=1, source_target_pairs={{0,1},{1,2},{2,3},{3,4},{4,5},{5,6},{6,7},{7,8},{8,9},{9,10},{10,1... | collective-permute-start | bytes 835592 | tf_op jit(solution)/shard_map/ppermute | solution.py:17
  59.5 8.2 %collective-permute-start.3 = (bf16[136,4,256]{2,0,1:T(8,128)(2,1)S(1)}, bf16[136,4,256]{2,0,1:T(8,128)(2,1)S(1)}, u32[]{:S(2)}, u32[]{:S(2)}) collective-permute-start(bf16[136,4,256]{2,0,1:T(8,128)(2,1)S(1)} %get-tuple-element.58), channel_id=1, source_target_pairs={{1,0},{2,1},{3,2},{4,3},{5,4},{6,5},{7,6},{8,7},{9,8},{10,9},{11,1... | collective-permute-start | bytes 835592 | tf_op jit(solution)/shard_map/ppermute | solution.py:18
  64.4 5.9 %copy-start.4 = (bf16[40,40]{1,0:T(8,128)(2,1)S(1)}, bf16[40,40]{1,0:T(8,128)(2,1)}, u32[]{:S(2)}) copy-start(bf16[40,40]{1,0:T(8,128)(2,1)} %param.26) | copy-start | bytes 9604
  70.3 6.0 %copy-start.13 = (f32[256]{0:T(256)S(1)}, f32[256]{0:T(256)}, u32[]{:S(2)}) copy-start(f32[256]{0:T(256)} %param.30) | copy-start | bytes 3076
  81.9 16.1 %collective-permute-start.4 = (bf16[4,40,256]{2,0,1:T(4,128)(2,1)S(1)}, bf16[4,40,256]{2,0,1:T(4,128)(2,1)S(1)}, u32[]{:S(2)}, u32[]{:S(2)}) collective-permute-start(bf16[4,40,256]{2,0,1:T(4,128)(2,1)S(1)} %get-tuple-element.53), channel_id=1, source_target_pairs={{0,32},{32,64},{64,96},{96,128},{128,160},{160,192},{192,224},{224... | collective-permute-start | bytes 245768 | tf_op jit(solution)/shard_map/ppermute | solution.py:17
  96.5 4.2 %collective-permute-start.5 = (bf16[4,40,256]{2,0,1:T(4,128)(2,1)S(1)}, bf16[4,40,256]{2,0,1:T(4,128)(2,1)S(1)}, u32[]{:S(2)}, u32[]{:S(2)}) collective-permute-start(bf16[4,40,256]{2,0,1:T(4,128)(2,1)S(1)} %get-tuple-element.54), channel_id=1, source_target_pairs={{32,0},{64,32},{96,64},{128,96},{160,128},{192,160},{224,192},{0,2... | collective-permute-start | bytes 245768 | tf_op jit(solution)/shard_map/ppermute | solution.py:18
  101.5 11.1 %collective-permute-start.6 = (bf16[128,4,256]{2,0,1:T(8,128)(2,1)S(1)}, bf16[128,4,256]{2,0,1:T(8,128)(2,1)S(1)}, u32[]{:S(2)}, u32[]{:S(2)}) collective-permute-start(bf16[128,4,256]{2,0,1:T(8,128)(2,1)S(1)} %get-tuple-element.55), channel_id=1, source_target_pairs={{0,1},{1,2},{2,3},{3,4},{4,5},{5,6},{6,7},{7,8},{8,9},{9,10},{10,1... | collective-permute-start | bytes 786440 | tf_op jit(solution)/shard_map/ppermute | solution.py:17
  101.5 11.0 %collective-permute-start.7 = (bf16[128,4,256]{2,0,1:T(8,128)(2,1)S(1)}, bf16[128,4,256]{2,0,1:T(8,128)(2,1)S(1)}, u32[]{:S(2)}, u32[]{:S(2)}) collective-permute-start(bf16[128,4,256]{2,0,1:T(8,128)(2,1)S(1)} %get-tuple-element.56), channel_id=1, source_target_pairs={{1,0},{2,1},{3,2},{4,3},{5,4},{6,5},{7,6},{8,7},{9,8},{10,9},{11,1... | collective-permute-start | bytes 786440 | tf_op jit(solution)/shard_map/ppermute | solution.py:18
